TPU v7x, 256 devices: a whole 4x4x8 slice. The times are simulated.
256 devices in a mesh: site: 16 (over z_hi, y, core), blk: 16 (over z_lo, x).
Axes of the slice: x: 4, y: 4, z: 8 (z_hi: 2, z_lo: 4; z = z_hi * 4 + z_lo), core: 2. Of those that a mesh axis runs over, the one named last changes fastest.
Arguments:
- corner: bfloat16 [16, 96, 128, 128], P('site', 'blk')
- bcorner: bfloat16 [2, 16, 96, 128, 128], P(None, 'site', 'blk'), may hold values from -6 to 6
- edge: bfloat16 [16, 96, 128, 2304], P('site', 'blk'), may hold values from -0.5 to 0.5
- bedge: bfloat16 [16, 96, 128, 2304], P('site', 'blk'), may hold values from -0.5 to 0.5
- proj: bfloat16 [16, 96, 2304, 128], P('site', 'blk'), may hold values from -0.125 to 0.125
- joining: int32 [16, 96], P('site'), may hold values from 0 to 95, as said below
- momentum: float32 [1], replicated, may hold values from 0.5 to 2.5
Outputs:
- new_corner: bfloat16 [16, 96, 128, 128], P('site', 'blk')
- new_bcorner: bfloat16 [2, 16, 96, 128, 128], P(None, 'site', 'blk')
- momentum_sum: float32 [2, 96, 128, 128], P(None, 'blk', 'site')
Inputs may be any that keep to these rules, and one draw needn't show every extreme that they name: Each row of joining is a permutation of the 96 slots. The 6 new slots of one blk device take their blocks from the slots of at most 3 blk devices, exactly 2 from each of them.
All inputs are finite; a program needn't handle non-finite values. Where the computation divides by a largest or mean magnitude, that divisor is 1e-20 or more.
Results may differ from a plain program's by a relative error of at most 0.024.
Values may be sent and summed in bfloat16 or wider, within the bound.
A program may use at most 128 MiB of HBM per device.

v0:
```python
import jax
import jax.numpy as jnp
from jax import lax
from jax.sharding import PartitionSpec as P

epsilon = 1e-06


def shifted(block, axis, distance):
    devices = range(lax.axis_size(axis))
    route = [((i - distance) % len(devices), i) for i in devices]
    return lax.ppermute(block, axis, route)


def product(left, right):
    return jnp.einsum("jmn,jnk->jmk", left, right, preferred_element_type=jnp.float32)


def per_device(corner, bcorner, edge, bedge, proj, joining, momentum):
    per_dev = corner.shape[1]
    my_blk = lax.axis_index("blk")
    my_site = lax.axis_index("site")
    left_corner, left_bcorner = shifted((corner, bcorner), "site", 1)
    corner_here = left_corner[0]
    column = edge[0]
    bcolumn = bedge[0]
    project = proj[0]
    enlarged = product(corner_here, column).astype(jnp.bfloat16)
    real_term = product(left_bcorner[0, 0], column)
    imag_term = product(left_bcorner[1, 0], column)
    inserted = product(corner_here, bcolumn)
    angle = momentum[0] * my_site.astype(jnp.float32)
    cosine = jnp.cos(angle)
    sine = jnp.sin(angle)
    excited_re = (cosine * real_term - sine * imag_term + inserted).astype(jnp.bfloat16)
    excited_im = (sine * real_term + cosine * imag_term).astype(jnp.bfloat16)
    projected = jnp.stack(
        [
            product(enlarged, project).astype(jnp.bfloat16),
            product(excited_re, project).astype(jnp.bfloat16),
            product(excited_im, project).astype(jnp.bfloat16),
        ],
        axis=1,
    )
    local_peak = jnp.max(jnp.abs(projected[:, 0].astype(jnp.float32)))
    peak = lax.pmax(local_peak, "blk")
    sources = lax.dynamic_slice_in_dim(joining[0], my_blk * per_dev, per_dev)
    piece = lax.all_gather(projected, "blk", axis=0, tiled=True)
    picks = (sources[:, None] == jnp.arange(piece.shape[0], dtype=jnp.int32)[None, :]).astype(
        jnp.bfloat16
    )
    routed = jnp.einsum("it,txmn->ixmn", picks, piece, preferred_element_type=jnp.float32)
    scaled = routed / (peak + epsilon)
    new_corner = scaled[:, 0].astype(jnp.bfloat16)
    new_b = jnp.stack([scaled[:, 1], scaled[:, 2]], axis=0).astype(jnp.bfloat16)
    summed = lax.psum_scatter(
        new_b.astype(jnp.float32).astype(jnp.bfloat16), "site", scatter_dimension=2, tiled=True
    ).astype(jnp.float32)
    return (new_corner[None], new_b[:, None], summed)


def solution(mesh):
    in_specs = (
        P("site", "blk", None, None),
        P(None, "site", "blk", None, None),
        P("site", "blk", None, None),
        P("site", "blk", None, None),
        P("site", "blk", None, None),
        P("site", None),
        P(),
    )
    out_specs = (
        P("site", "blk", None, None),
        P(None, "site", "blk", None, None),
        P(None, "blk", "site", None),
    )
    return jax.shard_map(
        per_device, mesh=mesh, in_specs=in_specs, out_specs=out_specs, check_vma=False
    )
```

profile of v0, /device:TPU:24, one launch (start us, length us, event | category | flops | bytes accessed | tf_op | source)
XLA Modules:
  0.0 357.3 jit_solution(6874294399947471244)
XLA Ops:
  7.2 0.1 collective-permute-start
  7.3 6.9 %collective-permute-start.1 = (bf16[2,1,6,128,128]{4,3,2,1,0:T(8,128)(2,1)}, bf16[2,1,6,128,128]{4,3,2,1,0:T(8,128)(2,1)}, u32[]{:S(2)}, u32[]{:S(2)}) collective-permute-start(bf16[2,1,6,128,128]{4,3,2,1,0:T(8,128)(2,1)} %param.8), channel_id=1, source_target_pairs={{240,0},{0,16},{16,32},{32,48},{48,64},{64,80},{80,96},{96,112},{1... | collective-permute-start | bytes 1179656 | tf_op jit(solution)/shard_map/ppermute | solution.py:12
  15.1 5.4 %abs_reduce_fusion = (f32[]{:T(128)}, bf16[6,128,128]{2,1,0:T(8,128)(2,1)}) fusion(bf16[1,6,2304,128]{3,2,1,0:T(8,128)(2,1)} %param.11, bf16[1,6,128,2304]{3,2,1,0:T(8,128)(2,1)S(1)} %copy-done, bf16[1,6,128,128]{3,2,1,0:T(8,128)(2,1)} %collective-permute-done), kind=kOutput, calls=%fused_computation.34 | convolution fusion | flops 908132352 | bytes 7471108 | tf_op jit(solution)/shard_map/jmn,jnk->jmk/dot_general | solution.py:16
  20.5 2.0 fusion.10
  22.5 2.2 fusion.12
  24.7 0.7 copy-done.1
  25.4 2.9 copy-done.2
  28.3 4.0 %fusion.43 = bf16[6,1,128,128]{3,2,0,1:T(8,128)(2,1)} fusion(bf16[1,6,2304,128]{3,2,1,0:T(8,128)(2,1)} %param.11, f32[6,128,2304]{2,1,0:T(8,128)S(1)} %fusion.10, f32[6,128,2304]{2,1,0:T(8,128)S(1)} %fusion.12, f32[]{:T(128)S(6)} %sin.3, f32[]{:T(128)S(6)} %cos.3), kind=kOutput, calls=%fused_computation.26 | convolution fusion | flops 460161024 | bytes 17891336 | tf_op jit(solution)/shard_map/jmn,jnk->jmk/dot_general | solution.py:16
  32.3 10.1 %fusion.38 = bf16[6,1,128,128]{3,2,0,1:T(8,128)(2,1)} fusion(bf16[1,6,2304,128]{3,2,1,0:T(8,128)(2,1)} %param.11, f32[6,128,2304]{2,1,0:T(8,128)} %copy-done.1, f32[6,128,2304]{2,1,0:T(8,128)} %copy-done.2, f32[]{:T(128)S(6)} %sin.3, f32[]{:T(128)S(6)} %cos.3, bf16[1,6,128,2304]{3,2,1,0:T(8,128)(2,1)} %param.10, ...), kind=kOutput, calls=%fused_computation.25 | convolution fusion | flops 914915328 | bytes 21626888 | tf_op jit(solution)/shard_map/jmn,jnk->jmk/dot_general | solution.py:16
  42.5 2.0 pad_maximum_fusion
  44.6 0.1 dynamic-slice_bitcast_fusion
  44.6 43.2 %pmax.7 = f32[]{:T(128)} all-reduce(f32[]{:T(128)} %get-tuple-element.14), channel_id=1, replica_groups=mesh['site'=16,'blk'=16] {'blk'}, use_global_device_ids=true, to_apply=%region_1.0 | all-reduce | flops 1 | bytes 8 | tf_op jit(solution)/shard_map/pmax | solution.py:46
  88.5 78.3 %all-gather.2.cloned.1.call-done = bf16[96,3,128,128]{3,2,0,1:T(8,128)(2,1)} async-done(((bf16[6,3,128,128]{3,2,0,1:T(8,128)(2,1)}), bf16[96,3,128,128]{3,2,0,1:T(8,128)(2,1)}) %all-gather.2.cloned.1.call-update) | async-done | bytes 9437200 | tf_op jit(solution)/shard_map/all_gather | solution.py:48
  166.8 8.8 %fusion.46 = bf16[6,3,128,128]{3,0,2,1:T(8,128)(2,1)S(1)} fusion(bf16[96,3,128,128]{3,2,0,1:T(8,128)(2,1)} %all-gather.2.cloned.1.call-done, f32[]{:T(128)S(6)} %add.17, s32[6]{0:T(128)S(1)} %dynamic-slice_bitcast_fusion), kind=kOutput, calls=%fused_computation.27 | convolution fusion | flops 57213504 | bytes 10027036 | tf_op jit(solution)/shard_map/it,txmn->ixmn/dot_general | solution.py:52
  175.6 1.0 fusion.54
  176.6 0.1 pad_maximum_fusion.2
  176.7 1.4 copy.15
  178.1 0.6 dynamic-slice.1
  179.4 1.2 pad_maximum_fusion.1
  180.5 0.8 copy.17
  181.3 1.7 copy.16
  183.0 166.1 %all-reduce.3.cloned.1.call-done = bf16[2,6,128,128]{3,0,1,2:T(2,128)(2,1)} async-done(((bf16[2,6,128,128]{3,0,1,2:T(2,128)(2,1)}), bf16[2,6,128,128]{3,0,1,2:T(2,128)(2,1)}) %all-reduce.3.cloned.1.call-update) | async-done | bytes 393232
  349.1 0.8 dynamic-slice_convert_fusion
  349.9 0.6 copy.18
  (14 shorter events, 0.1 us)
Async XLA Ops:
  7.2 7.9 %copy-start = (bf16[1,6,128,2304]{3,2,1,0:T(8,128)(2,1)S(1)}, bf16[1,6,128,2304]{3,2,1,0:T(8,128)(2,1)}, u32[]{:S(2)}) copy-start(bf16[1,6,128,2304]{3,2,1,0:T(8,128)(2,1)} %param.9) | copy-start | bytes 10616836
  7.2 159.6 %all-gather.2.cloned.1.call-start = ((), (), s32[]{:S(2)}) async-start(), calls=%async_computation | async-start | bytes 10027008 | tf_op jit(solution)/shard_map/all_gather | solution.py:48
  7.2 7.8 %collective-permute-start = (bf16[1,6,128,128]{3,2,1,0:T(8,128)(2,1)}, bf16[1,6,128,128]{3,2,1,0:T(8,128)(2,1)}, u32[]{:S(2)}, u32[]{:S(2)}) collective-permute-start(bf16[1,6,128,128]{3,2,1,0:T(8,128)(2,1)} %param.7), channel_id=1, source_target_pairs={{240,0},{0,16},{16,32},{32,48},{48,64},{64,80},{80,96},{96,112},{1... | collective-permute-start | bytes 589832 | tf_op jit(solution)/shard_map/ppermute | solution.py:12
  7.3 13.2 %collective-permute-start.1 = (bf16[2,1,6,128,128]{4,3,2,1,0:T(8,128)(2,1)}, bf16[2,1,6,128,128]{4,3,2,1,0:T(8,128)(2,1)}, u32[]{:S(2)}, u32[]{:S(2)}) collective-permute-start(bf16[2,1,6,128,128]{4,3,2,1,0:T(8,128)(2,1)} %param.8), channel_id=1, source_target_pairs={{240,0},{0,16},{16,32},{32,48},{48,64},{64,80},{80,96},{96,112},{1... | collective-permute-start | bytes 1179656 | tf_op jit(solution)/shard_map/ppermute | solution.py:12
  22.5 2.9 copy-start.1
  25.4 2.9 copy-start.2
  32.3 12.2 %copy-start.3 = (s32[1,96]{1,0:T(1,128)S(1)}, s32[1,96]{1,0:T(1,128)}, u32[]{:S(2)}) copy-start(s32[1,96]{1,0:T(1,128)} %param.12) | copy-start | bytes 1156
  44.5 304.6 %all-reduce.3.cloned.1.call-start = ((), (), s32[]{:S(2)}) async-start(), calls=%async_computation.1 | async-start | bytes 786432
  175.6 2.5 copy-start.4
Sparse Core Ops, SparseCore 0:
  44.6 122.1 all-gather.1
  178.2 170.8 all-reduce.2
where the time goes:
time: 361 us; the launch traced here: 357 us
  waiting for transfers between devices  244 us (68%)
  blocking collectives  43.2 us (12%)
  matrix products  32.5 us (9%)
  between operations  16.2 us (4%)
  local copies, waits for them, and re-layouts  9.75 us (3%)
  starting transfers between devices  7.11 us (2%)
  other arithmetic  4.03 us (1%)
    unnamed x3, waiting for transfers between devices  166 us
    all_gather x1, waiting for transfers between devices, per_device(): piece = lax.all_gather(projected, 'blk', axis=0, tiled=True)  78.3 us
    pmax x1, blocking collectives, per_device(): peak = lax.pmax(local_peak, 'blk')  43.2 us
    dot_general x5, matrix products, product(): jnp.einsum('jmn,jnk->jmk', left, right, preferred_element_type=jnp.float32)  23.7 us
    dot_general x1, matrix products, per_device(): jnp.einsum('it,txmn->ixmn', picks, piece, preferred_element_type=jnp.floa...  8.79 us
    unnamed x14, local copies, waits for them, and re-layouts  7.33 us
  transfers between devices with their start and end apart: 4, of which 2 were waited for; matrix products, arithmetic and copies ran while one was open for 3% of the time, Pallas kernels for 0%

commit v1 on v0

v1 whole, which is shorter than its diff:
```python
import functools

import jax
import jax.numpy as jnp
from jax import lax
from jax.experimental import pallas as pl
from jax.experimental.pallas import tpu as pltpu
from jax.sharding import PartitionSpec as P

EPS = 1e-6
MESH = pl.DeviceIdType.MESH
NX = 4
NZ = 4
BLOCKS = 3
ORDER = (1, 2, 0)
HALVES = 2


def mega(
    n_site,
    join_ref,
    mom_ref,
    corner_ref,
    bcorner_ref,
    edge_ref,
    bedge_ref,
    proj_ref,
    outc_ref,
    outb_ref,
    sum_ref,
    edge_v,
    bedge_v,
    proj_v,
    cb_v,
    e_v,
    d_v,
    peak_src,
    peak_all,
    msend,
    mrecv,
    tab,
    *rest,
):
    nb = edge_v.shape[0]
    m = cb_v.shape[-1]
    n_blk = NX * NZ
    rows = m // HALVES
    chunks = [(b, h) for b in ORDER for h in range(HALVES)]
    nc = len(chunks)
    gath = rest[:nc]
    xsend = rest[nc : 2 * nc]
    got = rest[2 * nc : 3 * nc]
    (load_sem, s_send, s_recv, z_up, z_down, z_recv, x_send, x_recv, p_send, p_recv, m_send, m_recv) = rest[
        3 * nc :
    ]

    site = lax.axis_index("site")
    blk = lax.axis_index("blk")
    z = blk // NX
    x = blk % NX

    def at(s, b):
        return {"site": s, "blk": b}

    barrier = pltpu.get_barrier_semaphore()
    for k in range(1, n_site):
        pl.semaphore_signal(barrier, inc=1, device_id=at((site + k) % n_site, blk), device_id_type=MESH)
    for k in range(1, n_blk):
        pl.semaphore_signal(barrier, inc=1, device_id=at(site, (blk + k) % n_blk), device_id_type=MESH)

    def loads(q):
        return [
            pltpu.make_async_copy(src.at[0, q], dst.at[q], load_sem.at[i, q])
            for i, (src, dst) in enumerate(((edge_ref, edge_v), (bedge_ref, bedge_v), (proj_ref, proj_v)))
        ]

    for q in range(nb):
        for copy in loads(q):
            copy.start()

    for dx in range(NX):
        target = z * NX + (x + dx) % NX
        for k in range(nb):
            src = join_ref[0, target * nb + k]
            dev = src // nb
            tab[dx * nb + k] = (dev // NX) * nb + (src - dev * nb)
            if dx == 0:
                tab[NX * nb + k] = (x - dev % NX + NX) % NX

    pl.semaphore_wait(barrier, n_site + n_blk - 2)

    right = (site + 1) % n_site
    shift = [
        pltpu.make_async_remote_copy(
            src_ref=corner_ref.at[0],
            dst_ref=cb_v.at[0],
            send_sem=s_send.at[0],
            recv_sem=s_recv.at[0],
            device_id=at(right, blk),
            device_id_type=MESH,
        )
    ] + [
        pltpu.make_async_remote_copy(
            src_ref=bcorner_ref.at[c, 0],
            dst_ref=cb_v.at[1 + c],
            send_sem=s_send.at[1 + c],
            recv_sem=s_recv.at[1 + c],
            device_id=at(right, blk),
            device_id_type=MESH,
        )
        for c in range(2)
    ]
    for copy in shift:
        copy.start()

    def local(q, carry):
        for copy in loads(q):
            copy.wait()
        both = jnp.concatenate([edge_v[q], bedge_v[q]], axis=0)
        prod = jnp.dot(both, proj_v[q], preferred_element_type=jnp.float32).astype(jnp.bfloat16)
        e_v[q] = prod[:m]
        d_v[q] = prod[m:]
        return carry

    lax.fori_loop(0, nb, local, 0)

    angle = jnp.full((8, m), mom_ref[0] * site.astype(jnp.float32), jnp.float32)
    cosine = jnp.cos(angle)[:1]
    sine = jnp.sin(angle)[:1]

    for copy in shift:
        copy.wait_recv()

    def join_slot(q, top):
        left = jnp.concatenate([cb_v[0, q], cb_v[1, q], cb_v[2, q]], axis=0)
        main = jnp.dot(left, e_v[q], preferred_element_type=jnp.float32)
        inserted = jnp.dot(cb_v[0, q], d_v[q], preferred_element_type=jnp.float32)
        real, imag = main[m : 2 * m], main[2 * m :]
        blocks = [
            main[:m].astype(jnp.bfloat16),
            (cosine * real - sine * imag + inserted).astype(jnp.bfloat16),
            (sine * real + cosine * imag).astype(jnp.bfloat16),
        ]
        for c, (b, h) in enumerate(chunks):
            gath[c][z * nb + q] = blocks[b][h * rows : (h + 1) * rows]
        return jnp.maximum(top, jnp.max(jnp.abs(blocks[0].astype(jnp.float32))))

    top = lax.fori_loop(0, nb, join_slot, jnp.float32(0.0))
    peak_src[...] = jnp.full(peak_src.shape, top, jnp.float32)

    peaks = [
        pltpu.make_async_remote_copy(
            src_ref=peak_src,
            dst_ref=peak_all.at[k - 1],
            send_sem=p_send.at[k - 1],
            recv_sem=p_recv.at[k - 1],
            device_id=at(site, (blk + k) % n_blk),
            device_id_type=MESH,
        )
        for k in range(1, n_blk)
    ]

    def hop(c, j, up):
        sems = z_up if up else z_down
        step = z - j if up else j - z
        view = gath[c].at[pl.ds(j * nb, nb)]
        return pltpu.make_async_remote_copy(
            src_ref=view,
            dst_ref=view,
            send_sem=sems.at[c, step],
            recv_sem=z_recv.at[c, j],
            device_id=at(site, blk + NX if up else blk - NX),
            device_id_type=MESH,
        )

    def relay(c, s):
        @pl.when(z - s >= 0)
        def _():
            if s > 0:
                hop(c, z - s, True).wait_recv()

            if s < NZ - 1:

                @pl.when(z < NZ - 1)
                def _():
                    hop(c, z - s, True).start()

        @pl.when(z + s <= NZ - 1)
        def _():
            if s > 0:
                hop(c, z + s, False).wait_recv()

            if s < NZ - 1:

                @pl.when(z > 0)
                def _():
                    hop(c, z + s, False).start()

    def cross(c, dx):
        return pltpu.make_async_remote_copy(
            src_ref=xsend[c].at[dx - 1],
            dst_ref=got[c].at[dx],
            send_sem=x_send.at[c, dx - 1],
            recv_sem=x_recv.at[c, dx - 1],
            device_id=at(site, z * NX + (x + dx) % NX),
            device_id_type=MESH,
        )

    def send_x(c):
        for dx in (2, 1, 3):
            for k in range(nb):
                xsend[c][dx - 1, k] = gath[c][tab[dx * nb + k]]
            cross(c, dx).start()
        for k in range(nb):
            got[c][0, k] = gath[c][tab[k]]

    state = {}

    def finish(c):
        b, h = chunks[c]
        for dx in (2, 1, 3):
            cross(c, dx).wait_recv()
        if "scale" not in state:
            for copy in peaks:
                copy.wait_recv()
            best = peak_src[...]
            for k in range(n_blk - 1):
                best = jnp.maximum(best, peak_all[k])
            state["scale"] = best[:1] + EPS
        scale = state["scale"]
        held = []
        for k in range(nb):
            value = got[c][tab[NX * nb + k], k].astype(jnp.float32) / scale
            if b == 0:
                outc_ref[0, k, pl.ds(h * rows, rows)] = value.astype(jnp.bfloat16)
            else:
                outb_ref[b - 1, 0, k, pl.ds(h * rows, rows)] = value.astype(jnp.bfloat16)
                held.append(value.reshape(rows // 8, 8, m))
        for j in range(len(held) // 2):
            pair = jnp.concatenate([held[2 * j], held[2 * j + 1]], axis=1)
            msend[b - 1, pl.ds(h * (rows // 8), rows // 8), j] = pair.astype(jnp.bfloat16)

    def spread(c, k):
        return pltpu.make_async_remote_copy(
            src_ref=msend.at[c, (site + k) % n_site],
            dst_ref=mrecv.at[c, k - 1],
            send_sem=m_send.at[c, k - 1],
            recv_sem=m_recv.at[c, k - 1],
            device_id=at((site + k) % n_site, blk),
            device_id_type=MESH,
        )

    for step in range(nc + NZ):
        for c in range(nc):
            stage = step - c
            if 0 <= stage < NZ:
                relay(c, stage)
                if stage == NZ - 1:
                    send_x(c)
            elif stage == NZ:
                finish(c)
                b, h = chunks[c]
                if b > 0 and h == HALVES - 1:
                    for k in (8, 7, 9, 6, 10, 5, 11, 4, 12, 3, 13, 2, 14, 1, 15):
                        spread(b - 1, k).start()
        if step == 0:
            for copy in peaks:
                copy.start()

    for c in range(2):
        total = msend[c, site].astype(jnp.float32)
        for k in range(1, n_site):
            spread(c, k).wait_recv()
            total = total + mrecv[c, k - 1].astype(jnp.float32)
        for j in range(nb // 2):
            sum_ref[c, 2 * j] = total[j, :8]
            sum_ref[c, 2 * j + 1] = total[j, 8:]

    for copy in shift:
        copy.wait_send()
    for copy in peaks:
        copy.wait_send()
    for c in range(nc):
        for s in range(NZ - 1):

            @pl.when(jnp.logical_and(z - s >= 0, z < NZ - 1))
            def _():
                hop(c, z - s, True).wait_send()

            @pl.when(jnp.logical_and(z + s <= NZ - 1, z > 0))
            def _():
                hop(c, z + s, False).wait_send()

        for dx in (1, 2, 3):
            cross(c, dx).wait_send()
    for c in range(2):
        for k in range(1, n_site):
            spread(c, k).wait_send()


def per_device(n_site, corner, bcorner, edge, bedge, proj, joining, momentum):
    _, nb, m, kdim = edge.shape
    rows = m // HALVES
    n_blk = NX * NZ
    nc = BLOCKS * HALVES
    bf = jnp.bfloat16
    hbm = pl.BlockSpec(memory_space=pl.ANY)
    smem = pl.BlockSpec(memory_space=pltpu.SMEM)
    vmem = pl.BlockSpec(memory_space=pltpu.VMEM)
    dma = pltpu.SemaphoreType.DMA
    return pl.pallas_call(
        functools.partial(mega, n_site),
        out_shape=(
            jax.ShapeDtypeStruct(corner.shape, bf),
            jax.ShapeDtypeStruct(bcorner.shape, bf),
            jax.ShapeDtypeStruct((2, nb, m // n_site, m), jnp.float32),
        ),
        in_specs=[smem, smem, hbm, hbm, hbm, hbm, hbm],
        out_specs=(vmem, vmem, vmem),
        scratch_shapes=[
            pltpu.VMEM((nb, m, kdim), bf),
            pltpu.VMEM((nb, m, kdim), bf),
            pltpu.VMEM((nb, kdim, m), bf),
            pltpu.VMEM((3, nb, m, m), bf),
            pltpu.VMEM((nb, m, m), bf),
            pltpu.VMEM((nb, m, m), bf),
            pltpu.VMEM((8, m), jnp.float32),
            pltpu.VMEM((n_blk - 1, 8, m), jnp.float32),
            pltpu.VMEM((2, n_site, nb // 2, 16, m), bf),
            pltpu.VMEM((2, n_site - 1, nb // 2, 16, m), bf),
            pltpu.SMEM(((NX + 1) * nb,), jnp.int32),
        ]
        + [pltpu.VMEM((NZ * nb, rows, m), bf)] * nc
        + [pltpu.VMEM((NX - 1, nb, rows, m), bf)] * nc
        + [pltpu.VMEM((NX, nb, rows, m), bf)] * nc
        + [
            dma((3, nb)),
            dma((3,)),
            dma((3,)),
            dma((nc, NZ - 1)),
            dma((nc, NZ - 1)),
            dma((nc, NZ)),
            dma((nc, NX - 1)),
            dma((nc, NX - 1)),
            dma((n_blk - 1,)),
            dma((n_blk - 1,)),
            dma((2, n_site - 1)),
            dma((2, n_site - 1)),
        ],
        compiler_params=pltpu.CompilerParams(
            collective_id=0, has_side_effects=True, vmem_limit_bytes=48 << 20
        ),
        name="column_move",
    )(joining, momentum, corner, bcorner, edge, bedge, proj)


def solution(mesh):
    in_specs = (
        P("site", "blk", None, None),
        P(None, "site", "blk", None, None),
        P("site", "blk", None, None),
        P("site", "blk", None, None),
        P("site", "blk", None, None),
        P("site", None),
        P(),
    )
    out_specs = (
        P("site", "blk", None, None),
        P(None, "site", "blk", None, None),
        P(None, "blk", "site", None),
    )
    return jax.shard_map(
        functools.partial(per_device, mesh.shape["site"]),
        mesh=mesh,
        in_specs=in_specs,
        out_specs=out_specs,
        check_vma=False,
    )
```

time: 361 us -> 88.8 us (0.25)
  waiting for transfers between devices: 244 us -> 0 us
  Pallas kernels: 0 us -> 80.6 us
  blocking collectives: 43.2 us -> 0 us
  matrix products: 32.5 us -> 0 us
  between operations: 16.2 us -> 1.3 us
  starting transfers between devices: 7.11 us -> 0 us
  other arithmetic: 4.03 us -> 0 us
    unnamed x3 -> x0, waiting for transfers between devices: 166 us -> none
    pallas_call x0 -> x1, Pallas kernels: none -> 80.6 us  [per_device(): pl.pallas_call(functools.partial(mega, n_site), out_shape=(jax.ShapeDtype...]
    all_gather x1 -> x0, waiting for transfers between devices: 78.3 us -> none  [per_device(): piece = lax.all_gather(projected, 'blk', axis=0, tiled=True)]
    pmax x1 -> x0, blocking collectives: 43.2 us -> none  [per_device(): peak = lax.pmax(local_peak, 'blk')]
    dot_general x6 -> x0, matrix products: 32.5 us -> none  [the longest x5 23.7 us: product(): jnp.einsum('jmn,jnk->jmk', left, right, preferred_element_type=jnp.float32)]
    ppermute x2 -> x0, starting transfers between devices: 7.03 us -> none  [shifted(): return lax.ppermute(block, axis, route)]
    unnamed x14 -> x11, local copies, waits for them, and re-layouts: 7.33 us -> 6.61 us
  transfers between devices with their start and end apart: 4 -> 0, of which waited for: 2 -> 0; matrix products, arithmetic and copies ran while one was open for 3% -> 0% of each run, Pallas kernels for 0% -> 0%
where the time goes in v1:
time: 88.8 us; the launch traced here: 88.6 us
  Pallas kernels  80.6 us (91%)
  local copies, waits for them, and re-layouts  6.61 us (7%)
  between operations  1.3 us (1%)
    pallas_call x1, Pallas kernels, per_device(): pl.pallas_call(functools.partial(mega, n_site), out_shape=(jax.ShapeDtype...  80.6 us
    unnamed x11, local copies, waits for them, and re-layouts  6.61 us

profile of v1, /device:TPU:24, one launch (start us, length us, event | category | flops | bytes accessed | tf_op | source)
XLA Modules:
  0.0 88.6 jit_solution(16303548999359746293)
XLA Ops:
  1.3 0.0 copy-start
  1.3 2.0 %copy-done = bf16[1,6,128,2304]{3,2,1,0:T(8,128)(2,1)S(1)} copy-done((bf16[1,6,128,2304]{3,2,1,0:T(8,128)(2,1)S(1)}, bf16[1,6,128,2304]{3,2,1,0:T(8,128)(2,1)}, u32[]{:S(2)}) %copy-start) | copy-done | bytes 3538968
  3.3 0.0 copy-start.1
  3.3 1.0 %copy-done.1 = bf16[2,1,6,128,128]{4,3,2,1,0:T(8,128)(2,1)S(1)} copy-done((bf16[2,1,6,128,128]{4,3,2,1,0:T(8,128)(2,1)S(1)}, bf16[2,1,6,128,128]{4,3,2,1,0:T(8,128)(2,1)}, u32[]{:S(2)}) %copy-start.1) | copy-done | bytes 393240
  4.3 0.0 copy-start.2
  4.3 0.9 %copy-done.2 = bf16[1,6,128,128]{3,2,1,0:T(8,128)(2,1)S(1)} copy-done((bf16[1,6,128,128]{3,2,1,0:T(8,128)(2,1)S(1)}, bf16[1,6,128,128]{3,2,1,0:T(8,128)(2,1)}, u32[]{:S(2)}) %copy-start.2) | copy-done | bytes 196632
  5.2 0.0 copy-start.3
  5.2 0.7 copy-done.3
  5.9 80.6 %column_move.1 = (bf16[1,6,128,128]{3,2,1,0:T(8,128)(2,1)S(1)}, bf16[2,1,6,128,128]{4,3,2,1,0:T(8,128)(2,1)S(1)}, f32[2,6,8,128]{3,2,1,0:T(8,128)S(1)}) custom-call(s32[1,96]{1,0:T(1,128)S(1)} %copy-done.3, f32[1]{0:T(128)S(6)} %copy.13.mom_ref, bf16[1,6,128,128]{3,2,1,0:T(8,128)(2,1)S(1)} %copy-done.2, bf16[2,1,6,128,128]{4,3,2,1,0:T(8,128)(2,1)S(1)} %copy-done.1, ...), custom_call_target="tpu_custom_call" | custom-call | tf_op jit(solution)/shard_map/column_move/pallas_call | solution.py:311
  86.5 0.7 copy.14
  87.2 0.7 copy.15
  87.9 0.6 copy.16
Async XLA Ops:
  1.3 2.0 %copy-start = (bf16[1,6,128,2304]{3,2,1,0:T(8,128)(2,1)S(1)}, bf16[1,6,128,2304]{3,2,1,0:T(8,128)(2,1)}, u32[]{:S(2)}) copy-start(bf16[1,6,128,2304]{3,2,1,0:T(8,128)(2,1)} %edge_ref.1) | copy-start | bytes 10616836
  3.3 1.0 %copy-start.1 = (bf16[2,1,6,128,128]{4,3,2,1,0:T(8,128)(2,1)S(1)}, bf16[2,1,6,128,128]{4,3,2,1,0:T(8,128)(2,1)}, u32[]{:S(2)}) copy-start(bf16[2,1,6,128,128]{4,3,2,1,0:T(8,128)(2,1)} %bcorner_ref.1) | copy-start | bytes 1179652
  4.3 0.9 %copy-start.2 = (bf16[1,6,128,128]{3,2,1,0:T(8,128)(2,1)S(1)}, bf16[1,6,128,128]{3,2,1,0:T(8,128)(2,1)}, u32[]{:S(2)}) copy-start(bf16[1,6,128,128]{3,2,1,0:T(8,128)(2,1)} %corner_ref.1) | copy-start | bytes 589828
  5.2 0.7 copy-start.3

commit v2 on v1

v2 whole, which is shorter than its diff:
```python
import functools

import jax
import jax.numpy as jnp
from jax import lax
from jax.experimental import pallas as pl
from jax.experimental.pallas import tpu as pltpu
from jax.sharding import PartitionSpec as P

EPS = 1e-6
MESH = pl.DeviceIdType.MESH
NX = 4
NZ = 4
HALVES = 2
CHUNKS = (
    (True, 0, (1, 2)),
    (False, 1, (1, 2)),
    (True, 0, (0,)),
    (False, 1, (0,)),
)


def mega(
    n_site,
    join_ref,
    mom_ref,
    corner_ref,
    bcorner_ref,
    edge_ref,
    bedge_ref,
    proj_ref,
    outc_ref,
    outb_ref,
    sum_ref,
    edge_v,
    bedge_v,
    proj_v,
    cb_v,
    e_v,
    d_v,
    peak_src,
    peak_x,
    peak_mid,
    peak_z,
    msend,
    mrecv,
    mpart,
    mcross,
    tab,
    jsm,
    *rest,
):
    nb = edge_v.shape[0]
    m = cb_v.shape[-1]
    rows = m // HALVES
    nc = len(CHUNKS)
    along_z = [chunk[0] for chunk in CHUNKS]
    n_near = n_site // 2
    gath = rest[:nc]
    parts = [rest[nc + 5 * i : nc + 5 * i + 5] for i in range(nc)]
    (load_sem, s_send, s_recv, z_up, z_down, z_recv, x_send, x_recv, up_send, up_recv, dn_send, dn_recv, p_send, p_recv, m_send, m_recv, c_send, c_recv, j_sem) = rest[
        6 * nc :
    ]

    site = lax.axis_index("site")
    blk = lax.axis_index("blk")
    z = blk // NX
    x = blk % NX

    def at(s, b):
        return {"site": s, "blk": b}

    barrier = pltpu.get_barrier_semaphore()
    near, far = site % n_near, site // n_near

    def mate(k):
        return at(far * n_near + (near + k) % n_near, blk)

    def row_mate(dx):
        return at(site, z * NX + (x + dx) % NX)

    def column_mate(dz):
        return at(site, (z + dz) % NZ * NX + x)

    right, left = at((site + 1) % n_site, blk), at((site + n_site - 1) % n_site, blk)
    across = at((site + n_near) % n_site, blk)
    partners = (
        [right, left, across]
        + [mate(k) for k in range(1, n_near)]
        + [row_mate(d) for d in range(1, NX)]
        + [column_mate(d) for d in range(1, NZ)]
    )
    for partner in partners:
        pl.semaphore_signal(barrier, inc=1, device_id=partner, device_id_type=MESH)

    def loads(q):
        return [
            pltpu.make_async_copy(src.at[0, q], dst.at[q], load_sem.at[i, q])
            for i, (src, dst) in enumerate(((edge_ref, edge_v), (bedge_ref, bedge_v), (proj_ref, proj_v)))
        ]

    fetch = pltpu.make_async_copy(join_ref, jsm, j_sem)
    fetch.start()
    for q in range(nb):
        for copy in loads(q):
            copy.start()

    base = (NX + 1) * nb
    fetch.wait()
    for dx in range(NX):
        target = z * NX + (x + dx) % NX
        for k in range(nb):
            src = jsm[0, target * nb + k]
            dev = src // nb
            tab[dx * nb + k] = (dev // NX) * nb + (src - dev * nb)
            if dx == 0:
                tab[NX * nb + k] = (x - dev % NX + NX) % NX
    for t in range(NZ):
        for k in range(nb):
            src = jsm[0, (t * NX + x) * nb + k]
            dev = src // nb
            tab[base + t * nb + k] = (dev % NX) * nb + (src - dev * nb)
            tab[base + (NZ + t) * nb + k] = dev // NX

    pl.semaphore_wait(barrier, len(partners))

    def shift(h):
        part = pl.ds(h * rows, rows)
        sources = [corner_ref.at[0, :, part]] + [bcorner_ref.at[c, 0, :, part] for c in range(2)]
        return [
            pltpu.make_async_remote_copy(
                src_ref=source,
                dst_ref=cb_v.at[h, c],
                send_sem=s_send.at[h, c],
                recv_sem=s_recv.at[h, c],
                device_id=right,
                device_id_type=MESH,
            )
            for c, source in enumerate(sources)
        ]

    for h in range(HALVES):
        for copy in shift(h):
            copy.start()

    def local(q, carry):
        for copy in loads(q):
            copy.wait()
        both = jnp.concatenate([edge_v[q], bedge_v[q]], axis=0)
        prod = jnp.dot(both, proj_v[q], preferred_element_type=jnp.float32).astype(jnp.bfloat16)
        e_v[q] = prod[:m]
        d_v[q] = prod[m:]
        return carry

    lax.fori_loop(0, nb, local, 0)

    angle = jnp.full((8, m), mom_ref[0] * site.astype(jnp.float32), jnp.float32)
    cosine = jnp.cos(angle)[:1]
    sine = jnp.sin(angle)[:1]

    def join(h, top):
        for copy in shift(h):
            copy.wait_recv()

        def join_slot(q, top):
            left_rows = jnp.concatenate([cb_v[h, 0, q], cb_v[h, 1, q], cb_v[h, 2, q]], axis=0)
            main = jnp.dot(left_rows, e_v[q], preferred_element_type=jnp.float32)
            inserted = jnp.dot(cb_v[h, 0, q], d_v[q], preferred_element_type=jnp.float32)
            real, imag = main[rows : 2 * rows], main[2 * rows :]
            blocks = [
                main[:rows].astype(jnp.bfloat16),
                (cosine * real - sine * imag + inserted).astype(jnp.bfloat16),
                (sine * real + cosine * imag).astype(jnp.bfloat16),
            ]
            for c, (zfirst, half, held) in enumerate(CHUNKS):
                if half == h:
                    for i, b in enumerate(held):
                        gath[c][(z if zfirst else x) * nb + q, pl.ds(i * rows, rows)] = blocks[b]
            return jnp.maximum(top, jnp.max(jnp.abs(blocks[0].astype(jnp.float32))))

        return lax.fori_loop(0, nb, join_slot, top)

    peaks_x = [
        pltpu.make_async_remote_copy(
            src_ref=peak_src,
            dst_ref=peak_x.at[d - 1],
            send_sem=p_send.at[0, d - 1],
            recv_sem=p_recv.at[0, d - 1],
            device_id=row_mate(d),
            device_id_type=MESH,
        )
        for d in range(1, NX)
    ]
    peaks_z = [
        pltpu.make_async_remote_copy(
            src_ref=peak_mid,
            dst_ref=peak_z.at[d - 1],
            send_sem=p_send.at[1, d - 1],
            recv_sem=p_recv.at[1, d - 1],
            device_id=column_mate(d),
            device_id_type=MESH,
        )
        for d in range(1, NZ)
    ]

    def hop(c, j, up):
        sems = z_up if up else z_down
        step = z - j if up else j - z
        view = gath[c].at[pl.ds(j * nb, nb)]
        return pltpu.make_async_remote_copy(
            src_ref=view,
            dst_ref=view,
            send_sem=sems.at[c, step],
            recv_sem=z_recv.at[c, j],
            device_id=at(site, blk + NX if up else blk - NX),
            device_id_type=MESH,
        )

    def relay(c, s):
        @pl.when(z - s >= 0)
        def _():
            if s > 0:
                hop(c, z - s, True).wait_recv()

            if s < NZ - 1:

                @pl.when(z < NZ - 1)
                def _():
                    hop(c, z - s, True).start()

        @pl.when(z + s <= NZ - 1)
        def _():
            if s > 0:
                hop(c, z + s, False).wait_recv()

            if s < NZ - 1:

                @pl.when(z > 0)
                def _():
                    hop(c, z + s, False).start()

    def cross(c, dx):
        xsend, got = parts[c][:2]
        return pltpu.make_async_remote_copy(
            src_ref=xsend.at[dx - 1],
            dst_ref=got.at[dx],
            send_sem=x_send.at[c, dx - 1],
            recv_sem=x_recv.at[c, dx - 1],
            device_id=row_mate(dx),
            device_id_type=MESH,
        )

    def send_x(c):
        xsend, got = parts[c][:2]
        for dx in (2, 1, 3):
            for k in range(nb):
                xsend[dx - 1, k] = gath[c][tab[dx * nb + k]]
            cross(c, dx).start()
        for k in range(nb):
            got[0, k] = gath[c][tab[k]]

    def share(c, dx, owner):
        view = gath[c].at[pl.ds(owner * nb, nb)]
        return pltpu.make_async_remote_copy(
            src_ref=view,
            dst_ref=view,
            send_sem=x_send.at[c, dx - 1],
            recv_sem=x_recv.at[c, dx - 1],
            device_id=row_mate(dx),
            device_id_type=MESH,
        )

    def climb(c, t, up, last):
        out, inn, fin = parts[c][0 if up else 1], parts[c][2 if up else 3], parts[c][4]
        return pltpu.make_async_remote_copy(
            src_ref=out.at[t],
            dst_ref=fin.at[1 if up else 2] if last else inn.at[t],
            send_sem=(up_send if up else dn_send).at[c, t],
            recv_sem=(up_recv if up else dn_recv).at[c, t],
            device_id=at(site, blk + NX if up else blk - NX),
            device_id_type=MESH,
        )

    def flow(c, j, up):
        out, inn = parts[c][0 if up else 1], parts[c][2 if up else 3]
        first = j == (0 if up else NZ - 1)
        for t in range(NZ - 1, j, -1) if up else range(j):
            if not first:
                climb(c, t, up, False).wait_recv()
            for k in range(nb):
                mine = gath[c][tab[base + t * nb + k]]
                if not first:
                    mine = lax.select(tab[base + (NZ + t) * nb + k] == j, mine, inn[t, k])
                out[t, k] = mine
            climb(c, t, up, abs(t - j) == 1).start()

    def row_stage(c, stage):
        if stage == 0:
            for dx in (2, 1, 3):
                share(c, dx, x).start()
            return
        if stage == 1:
            for dx in (2, 1, 3):
                share(c, dx, (x + NX - dx) % NX).wait_recv()
        j = stage - 1
        if j < NZ - 1:

            @pl.when(z == j)
            def _():
                flow(c, j, True)

            @pl.when(z == NZ - 1 - j)
            def _():
                flow(c, NZ - 1 - j, False)

    def row_end(c):
        fin = parts[c][4]
        for k in range(nb):
            fin[0, k] = gath[c][tab[base + z * nb + k]]

        @pl.when(z > 0)
        def _():
            climb(c, z, True, True).wait_recv()

        @pl.when(z < NZ - 1)
        def _():
            climb(c, z, False, True).wait_recv()

    def picked(c, k):
        if along_z[c]:
            return parts[c][1][tab[NX * nb + k], k]
        source = tab[base + (NZ + z) * nb + k]
        which = jnp.where(source == z, 0, jnp.where(source < z, 1, 2))
        return parts[c][4][which, k]

    state = {}

    def finish(c):
        zfirst, h, blocks = CHUNKS[c]
        if zfirst:
            for dx in (2, 1, 3):
                cross(c, dx).wait_recv()
        else:
            row_end(c)
        if "scale" not in state:
            best = peak_mid[...]
            for d, copy in enumerate(peaks_z):
                copy.wait_recv()
                best = jnp.maximum(best, peak_z[d])
            state["scale"] = best[:1] + EPS
        scale = state["scale"]
        held = {b: [] for b in blocks}
        for k in range(nb):
            value = picked(c, k).astype(jnp.float32) / scale
            for i, b in enumerate(blocks):
                block = value[i * rows : (i + 1) * rows]
                if b == 0:
                    outc_ref[0, k, pl.ds(h * rows, rows)] = block.astype(jnp.bfloat16)
                else:
                    outb_ref[b - 1, 0, k, pl.ds(h * rows, rows)] = block.astype(jnp.bfloat16)
                    held[b].append(block.reshape(rows // 8, 8, m))
        per = rows // 8
        for b in blocks:
            if b == 0:
                continue
            for j in range(nb // 2):
                pair = jnp.concatenate([held[b][2 * j], held[b][2 * j + 1]], axis=1).astype(jnp.bfloat16)
                for f in range(2):
                    lo, hi = max(h * per, f * n_near), min((h + 1) * per, (f + 1) * n_near)
                    if lo < hi:
                        msend[f, pl.ds(lo - f * n_near, hi - lo), b - 1, j] = pair[lo - h * per : hi - h * per]

    def spread(k):
        return pltpu.make_async_remote_copy(
            src_ref=msend.at[:, (near + k) % n_near],
            dst_ref=mrecv.at[k - 1],
            send_sem=m_send.at[k - 1],
            recv_sem=m_recv.at[k - 1],
            device_id=mate(k),
            device_id_type=MESH,
        )

    over = pltpu.make_async_remote_copy(
        src_ref=mpart,
        dst_ref=mcross,
        send_sem=c_send,
        recv_sem=c_recv,
        device_id=across,
        device_id_type=MESH,
    )

    def near_sum():
        for k in range(1, n_near):
            spread(k).wait_recv()

        def total(f):
            value = msend[f, near].astype(jnp.float32)
            for k in range(1, n_near):
                value = value + mrecv[k - 1, f].astype(jnp.float32)
            return value

        mpart[...] = total(1 - far).astype(jnp.bfloat16)
        over.start()
        for c in range(2):
            kept = total(far)[c]
            for j in range(nb // 2):
                sum_ref[c, 2 * j] = kept[j, :8]
                sum_ref[c, 2 * j + 1] = kept[j, 8:]

    def far_sum():
        over.wait_recv()
        for c in range(2):
            for j in range(nb // 2):
                other = mcross[c, j].astype(jnp.float32)
                sum_ref[c, 2 * j] += other[:8]
                sum_ref[c, 2 * j + 1] += other[8:]

    last_b = max(c for c in range(nc) if CHUNKS[c][2] != (0,))
    top = join(0, jnp.float32(0.0))
    for step in range(nc + NZ):
        if step == 1:
            top = join(1, top)
            peak_src[...] = jnp.full(peak_src.shape, top, jnp.float32)
            for copy in peaks_x:
                copy.start()
        for c in range(nc):
            stage = step - c
            if 0 <= stage < NZ:
                if along_z[c]:
                    relay(c, stage)
                    if stage == NZ - 1:
                        send_x(c)
                else:
                    row_stage(c, stage)
            elif stage == NZ:
                if c == nc - 1:
                    near_sum()
                finish(c)
                if c == last_b:
                    for k in (4, 3, 5, 2, 6, 1, 7):
                        spread(k).start()
        if step == 2:
            best = peak_src[...]
            for d, copy in enumerate(peaks_x):
                copy.wait_recv()
                best = jnp.maximum(best, peak_x[d])
            peak_mid[...] = best
            for copy in peaks_z:
                copy.start()
    far_sum()

    for h in range(HALVES):
        for copy in shift(h):
            copy.wait_send()
    for copy in peaks_x + peaks_z:
        copy.wait_send()
    for c in range(nc):
        if not along_z[c]:
            for dx in (1, 2, 3):
                share(c, dx, x).wait_send()
            for t in range(NZ):

                @pl.when(z < t)
                def _():
                    climb(c, t, True, False).wait_send()

                @pl.when(z > t)
                def _():
                    climb(c, t, False, False).wait_send()

            continue
        for s in range(NZ - 1):

            @pl.when(jnp.logical_and(z - s >= 0, z < NZ - 1))
            def _():
                hop(c, z - s, True).wait_send()

            @pl.when(jnp.logical_and(z + s <= NZ - 1, z > 0))
            def _():
                hop(c, z + s, False).wait_send()

        for dx in (1, 2, 3):
            cross(c, dx).wait_send()
    for k in range(1, n_near):
        spread(k).wait_send()
    over.wait_send()


def per_device(n_site, corner, bcorner, edge, bedge, proj, joining, momentum):
    _, nb, m, kdim = edge.shape
    rows = m // HALVES
    nc = len(CHUNKS)
    tall = [rows * len(blocks) for _, _, blocks in CHUNKS]
    n_near = n_site // 2
    bf = jnp.bfloat16
    hbm = pl.BlockSpec(memory_space=pl.ANY)
    smem = pl.BlockSpec(memory_space=pltpu.SMEM)
    vmem = pl.BlockSpec(memory_space=pltpu.VMEM)
    dma = pltpu.SemaphoreType.DMA
    return pl.pallas_call(
        functools.partial(mega, n_site),
        out_shape=(
            jax.ShapeDtypeStruct(corner.shape, bf),
            jax.ShapeDtypeStruct(bcorner.shape, bf),
            jax.ShapeDtypeStruct((2, nb, m // n_site, m), jnp.float32),
        ),
        in_specs=[hbm, smem, hbm, hbm, hbm, hbm, hbm],
        out_specs=(vmem, vmem, vmem),
        scratch_shapes=[
            pltpu.VMEM((nb, m, kdim), bf),
            pltpu.VMEM((nb, m, kdim), bf),
            pltpu.VMEM((nb, kdim, m), bf),
            pltpu.VMEM((HALVES, 3, nb, rows, m), bf),
            pltpu.VMEM((nb, m, m), bf),
            pltpu.VMEM((nb, m, m), bf),
            pltpu.VMEM((8, m), jnp.float32),
            pltpu.VMEM((NX - 1, 8, m), jnp.float32),
            pltpu.VMEM((8, m), jnp.float32),
            pltpu.VMEM((NZ - 1, 8, m), jnp.float32),
            pltpu.VMEM((2, n_near, 2, nb // 2, 16, m), bf),
            pltpu.VMEM((n_near - 1, 2, 2, nb // 2, 16, m), bf),
            pltpu.VMEM((2, nb // 2, 16, m), bf),
            pltpu.VMEM((2, nb // 2, 16, m), bf),
            pltpu.SMEM(((NX + 1 + 2 * NZ) * nb,), jnp.int32),
            pltpu.SMEM(joining.shape, jnp.int32),
        ]
        + [pltpu.VMEM((NZ * nb, t, m), bf) for t in tall]
        + [pltpu.VMEM((NZ, nb, t, m), bf) for t in tall for _ in range(5)]
        + [
            dma((3, nb)),
            dma((HALVES, 3)),
            dma((HALVES, 3)),
            dma((nc, NZ - 1)),
            dma((nc, NZ - 1)),
            dma((nc, NZ)),
            dma((nc, NX - 1)),
            dma((nc, NX - 1)),
            dma((nc, NZ)),
            dma((nc, NZ)),
            dma((nc, NZ)),
            dma((nc, NZ)),
            dma((2, NX - 1)),
            dma((2, NX - 1)),
            dma((n_near - 1,)),
            dma((n_near - 1,)),
            dma,
            dma,
            dma,
        ],
        compiler_params=pltpu.CompilerParams(
            collective_id=0, has_side_effects=True, vmem_limit_bytes=62 << 20
        ),
        name="column_move",
    )(joining, momentum, corner, bcorner, edge, bedge, proj)


def solution(mesh):
    in_specs = (
        P("site", "blk", None, None),
        P(None, "site", "blk", None, None),
        P("site", "blk", None, None),
        P("site", "blk", None, None),
        P("site", "blk", None, None),
        P("site", None),
        P(),
    )
    out_specs = (
        P("site", "blk", None, None),
        P(None, "site", "blk", None, None),
        P(None, "blk", "site", None),
    )
    return jax.shard_map(
        functools.partial(per_device, mesh.shape["site"]),
        mesh=mesh,
        in_specs=in_specs,
        out_specs=out_specs,
        check_vma=False,
    )
```

time: 88.8 us -> 80.8 us (0.910)
  Pallas kernels: 80.6 us -> 74.5 us
  local copies, waits for them, and re-layouts: 6.61 us -> 4.8 us
    pallas_call x1, Pallas kernels: 80.6 us -> 74.5 us  [per_device(): pl.pallas_call(functools.partial(mega, n_site), out_shape=(jax.ShapeDtype...]
    unnamed x11 -> x3, local copies, waits for them, and re-layouts: 6.61 us -> 4.8 us
where the time goes in v2:
time: 80.8 us; the launch traced here: 80.6 us
  Pallas kernels  74.5 us (92%)
  local copies, waits for them, and re-layouts  4.8 us (6%)
  between operations  1.29 us (2%)
    pallas_call x1, Pallas kernels, per_device(): pl.pallas_call(functools.partial(mega, n_site), out_shape=(jax.ShapeDtype...  74.5 us
    unnamed x3, local copies, waits for them, and re-layouts  4.8 us

profile of v2, /device:TPU:24, one launch (start us, length us, event | category | flops | bytes accessed | tf_op | source)
XLA Modules:
  0.0 80.6 jit_solution(8674969235285501790)
XLA Ops:
  1.3 74.5 %column_move.1 = (bf16[1,6,128,128]{3,2,1,0:T(8,128)(2,1)}, bf16[2,1,6,128,128]{4,3,2,1,0:T(8,128)(2,1)}, f32[2,6,8,128]{3,2,1,0:T(8,128)}) custom-call(s32[1,96]{1,0:T(1,128)} %join_ref.1, f32[1]{0:T(128)S(6)} %copy.13.mom_ref, bf16[1,6,128,128]{3,2,1,0:T(8,128)(2,1)} %corner_ref.1, bf16[2,1,6,128,128]{4,3,2,1,0:T(8,128)(2,1)} %bcorner_ref.1, ...), custom_call_target="tpu_custom_call" | custom-call | tf_op jit(solution)/shard_map/column_move/pallas_call | solution.py:500
  75.8 1.6 %copy.14 = bf16[1,6,128,128]{3,2,1,0:T(8,128)(2,1)} copy(bf16[1,6,128,128]{3,2,1,0:T(8,128)(2,1)} %get-tuple-element.6) | data formatting | bytes 393216
  77.4 1.8 %copy.15 = bf16[2,1,6,128,128]{4,3,2,1,0:T(8,128)(2,1)} copy(bf16[2,1,6,128,128]{4,3,2,1,0:T(8,128)(2,1)} %get-tuple-element.7) | data formatting | bytes 786432
  79.2 1.4 %copy.16 = f32[2,6,8,128]{3,2,1,0:T(8,128)} copy(f32[2,6,8,128]{3,2,1,0:T(8,128)} %get-tuple-element.8) | data formatting | bytes 98304

commit v3 on v2

--- a/solution.py
+++ b/solution.py
@@ -13,10 +13,12 @@
 NZ = 4
 HALVES = 2
 CHUNKS = (
-    (True, 0, (1, 2)),
-    (False, 1, (1, 2)),
-    (True, 0, (0,)),
-    (False, 1, (0,)),
+    (True, 0, (1,), 0),
+    (False, 0, (2,), 0),
+    (True, 0, (0,), 1),
+    (False, 1, (1,), 1),
+    (True, 1, (2,), 1),
+    (False, 1, (0,), 2),
 )
 
 
@@ -172,7 +174,7 @@
                 (cosine * real - sine * imag + inserted).astype(jnp.bfloat16),
                 (sine * real + cosine * imag).astype(jnp.bfloat16),
             ]
-            for c, (zfirst, half, held) in enumerate(CHUNKS):
+            for c, (zfirst, half, held, _) in enumerate(CHUNKS):
                 if half == h:
                     for i, b in enumerate(held):
                         gath[c][(z if zfirst else x) * nb + q, pl.ds(i * rows, rows)] = blocks[b]
@@ -336,7 +338,7 @@
     state = {}
 
     def finish(c):
-        zfirst, h, blocks = CHUNKS[c]
+        zfirst, h, blocks, _ = CHUNKS[c]
         if zfirst:
             for dx in (2, 1, 3):
                 cross(c, dx).wait_recv()
@@ -417,14 +419,14 @@
 
     last_b = max(c for c in range(nc) if CHUNKS[c][2] != (0,))
     top = join(0, jnp.float32(0.0))
-    for step in range(nc + NZ):
+    for step in range(max(chunk[3] for chunk in CHUNKS) + NZ + 1):
         if step == 1:
             top = join(1, top)
             peak_src[...] = jnp.full(peak_src.shape, top, jnp.float32)
             for copy in peaks_x:
                 copy.start()
         for c in range(nc):
-            stage = step - c
+            stage = step - CHUNKS[c][3]
             if 0 <= stage < NZ:
                 if along_z[c]:
                     relay(c, stage)
@@ -490,7 +492,7 @@
     _, nb, m, kdim = edge.shape
     rows = m // HALVES
     nc = len(CHUNKS)
-    tall = [rows * len(blocks) for _, _, blocks in CHUNKS]
+    tall = [rows * len(chunk[2]) for chunk in CHUNKS]
     n_near = n_site // 2
     bf = jnp.bfloat16
     hbm = pl.BlockSpec(memory_space=pl.ANY)

time: 80.8 us -> 73.9 us (0.915)
  the two profiles are of different devices: /device:TPU:24 before, /device:TPU:16 now
where the time goes in v3:
time: 73.9 us; the launch traced here: 73.7 us
  Pallas kernels  67.6 us (91%)
  local copies, waits for them, and re-layouts  4.8 us (6%)
  between operations  1.29 us (2%)
    pallas_call x1, Pallas kernels, per_device(): pl.pallas_call(functools.partial(mega, n_site), out_shape=(jax.ShapeDtype...  67.6 us
    unnamed x3, local copies, waits for them, and re-layouts  4.8 us

profile of v3, /device:TPU:16, one launch (start us, length us, event | category | flops | bytes accessed | tf_op | source)
XLA Modules:
  0.0 73.7 jit_solution(16800314053707983866)
XLA Ops:
  1.3 67.6 %column_move.1 = (bf16[1,6,128,128]{3,2,1,0:T(8,128)(2,1)}, bf16[2,1,6,128,128]{4,3,2,1,0:T(8,128)(2,1)}, f32[2,6,8,128]{3,2,1,0:T(8,128)}) custom-call(s32[1,96]{1,0:T(1,128)} %join_ref.1, f32[1]{0:T(128)S(6)} %copy.13.mom_ref, bf16[1,6,128,128]{3,2,1,0:T(8,128)(2,1)} %corner_ref.1, bf16[2,1,6,128,128]{4,3,2,1,0:T(8,128)(2,1)} %bcorner_ref.1, ...), custom_call_target="tpu_custom_call" | custom-call | tf_op jit(solution)/shard_map/column_move/pallas_call | solution.py:502
  68.9 1.6 %copy.14 = bf16[1,6,128,128]{3,2,1,0:T(8,128)(2,1)} copy(bf16[1,6,128,128]{3,2,1,0:T(8,128)(2,1)} %get-tuple-element.6) | data formatting | bytes 393216
  70.5 1.8 %copy.15 = bf16[2,1,6,128,128]{4,3,2,1,0:T(8,128)(2,1)} copy(bf16[2,1,6,128,128]{4,3,2,1,0:T(8,128)(2,1)} %get-tuple-element.7) | data formatting | bytes 786432
  72.3 1.4 %copy.16 = f32[2,6,8,128]{3,2,1,0:T(8,128)} copy(f32[2,6,8,128]{3,2,1,0:T(8,128)} %get-tuple-element.8) | data formatting | bytes 98304

commit v4 on v3

--- a/solution.py
+++ b/solution.py
@@ -15,9 +15,9 @@
 CHUNKS = (
     (True, 0, (1,), 0),
     (False, 0, (2,), 0),
-    (True, 0, (0,), 1),
     (False, 1, (1,), 1),
     (True, 1, (2,), 1),
+    (True, 0, (0,), 1),
     (False, 1, (0,), 2),
 )
 
@@ -372,12 +372,12 @@
                     if lo < hi:
                         msend[f, pl.ds(lo - f * n_near, hi - lo), b - 1, j] = pair[lo - h * per : hi - h * per]
 
-    def spread(k):
+    def spread(f, k):
         return pltpu.make_async_remote_copy(
-            src_ref=msend.at[:, (near + k) % n_near],
-            dst_ref=mrecv.at[k - 1],
-            send_sem=m_send.at[k - 1],
-            recv_sem=m_recv.at[k - 1],
+            src_ref=msend.at[f, (near + k) % n_near],
+            dst_ref=mrecv.at[f, k - 1],
+            send_sem=m_send.at[f, k - 1],
+            recv_sem=m_recv.at[f, k - 1],
             device_id=mate(k),
             device_id_type=MESH,
         )
@@ -391,23 +391,23 @@
         device_id_type=MESH,
     )
 
-    def near_sum():
+    def near_sum(f):
+        total = msend[f, near].astype(jnp.float32)
         for k in range(1, n_near):
-            spread(k).wait_recv()
-
-        def total(f):
-            value = msend[f, near].astype(jnp.float32)
-            for k in range(1, n_near):
-                value = value + mrecv[k - 1, f].astype(jnp.float32)
-            return value
-
-        mpart[...] = total(1 - far).astype(jnp.bfloat16)
-        over.start()
-        for c in range(2):
-            kept = total(far)[c]
-            for j in range(nb // 2):
-                sum_ref[c, 2 * j] = kept[j, :8]
-                sum_ref[c, 2 * j + 1] = kept[j, 8:]
+            spread(f, k).wait_recv()
+            total = total + mrecv[f, k - 1].astype(jnp.float32)
+
+        @pl.when(far == f)
+        def _():
+            for c in range(2):
+                for j in range(nb // 2):
+                    sum_ref[c, 2 * j] = total[c, j, :8]
+                    sum_ref[c, 2 * j + 1] = total[c, j, 8:]
+
+        @pl.when(far != f)
+        def _():
+            mpart[...] = total.astype(jnp.bfloat16)
+            over.start()
 
     def far_sum():
         over.wait_recv()
@@ -417,7 +417,7 @@
                 sum_ref[c, 2 * j] += other[:8]
                 sum_ref[c, 2 * j + 1] += other[8:]
 
-    last_b = max(c for c in range(nc) if CHUNKS[c][2] != (0,))
+    last_b = [max(c for c in range(nc) if CHUNKS[c][1] == h and CHUNKS[c][2] != (0,)) for h in range(HALVES)]
     top = join(0, jnp.float32(0.0))
     for step in range(max(chunk[3] for chunk in CHUNKS) + NZ + 1):
         if step == 1:
@@ -434,13 +434,18 @@
                         send_x(c)
                 else:
                     row_stage(c, stage)
-            elif stage == NZ:
+        for c in range(nc):
+            stage = step - CHUNKS[c][3]
+            if stage == NZ:
                 if c == nc - 1:
-                    near_sum()
+                    near_sum(1)
                 finish(c)
-                if c == last_b:
-                    for k in (4, 3, 5, 2, 6, 1, 7):
-                        spread(k).start()
+                for f in range(HALVES):
+                    if c == last_b[f]:
+                        for k in (4, 3, 5, 2, 6, 1, 7):
+                            spread(f, k).start()
+                if c == last_b[1]:
+                    near_sum(0)
         if step == 2:
             best = peak_src[...]
             for d, copy in enumerate(peaks_x):
@@ -483,9 +488,19 @@
 
         for dx in (1, 2, 3):
             cross(c, dx).wait_send()
-    for k in range(1, n_near):
-        spread(k).wait_send()
+    for f in range(HALVES):
+        for k in range(1, n_near):
+            spread(f, k).wait_send()
     over.wait_send()
+
+
+def store(*refs):
+    n = (len(refs) - 1) // 2
+    copies = [pltpu.make_async_copy(refs[i], refs[n + i], refs[-1].at[i]) for i in range(n)]
+    for copy in copies:
+        copy.start()
+    for copy in copies:
+        copy.wait()
 
 
 def per_device(n_site, corner, bcorner, edge, bedge, proj, joining, momentum):
@@ -499,7 +514,7 @@
     smem = pl.BlockSpec(memory_space=pltpu.SMEM)
     vmem = pl.BlockSpec(memory_space=pltpu.VMEM)
     dma = pltpu.SemaphoreType.DMA
-    return pl.pallas_call(
+    results = pl.pallas_call(
         functools.partial(mega, n_site),
         out_shape=(
             jax.ShapeDtypeStruct(corner.shape, bf),
@@ -520,7 +535,7 @@
             pltpu.VMEM((8, m), jnp.float32),
             pltpu.VMEM((NZ - 1, 8, m), jnp.float32),
             pltpu.VMEM((2, n_near, 2, nb // 2, 16, m), bf),
-            pltpu.VMEM((n_near - 1, 2, 2, nb // 2, 16, m), bf),
+            pltpu.VMEM((2, n_near - 1, 2, nb // 2, 16, m), bf),
             pltpu.VMEM((2, nb // 2, 16, m), bf),
             pltpu.VMEM((2, nb // 2, 16, m), bf),
             pltpu.SMEM(((NX + 1 + 2 * NZ) * nb,), jnp.int32),
@@ -543,8 +558,8 @@
             dma((nc, NZ)),
             dma((2, NX - 1)),
             dma((2, NX - 1)),
-            dma((n_near - 1,)),
-            dma((n_near - 1,)),
+            dma((2, n_near - 1)),
+            dma((2, n_near - 1)),
             dma,
             dma,
             dma,
@@ -554,6 +569,14 @@
         ),
         name="column_move",
     )(joining, momentum, corner, bcorner, edge, bedge, proj)
+    return pl.pallas_call(
+        store,
+        out_shape=tuple(jax.ShapeDtypeStruct(r.shape, r.dtype) for r in results),
+        in_specs=[vmem] * len(results),
+        out_specs=tuple(hbm for _ in results),
+        scratch_shapes=[dma((len(results),))],
+        name="store",
+    )(*results)
 
 
 def solution(mesh):

time: 73.9 us -> 66.6 us (0.901)
  the two profiles are of different devices: /device:TPU:16 before, /device:TPU:1 now
where the time goes in v4:
time: 66.6 us; the launch traced here: 66.5 us
  Pallas kernels  65.2 us (98%)
  between operations  1.29 us (2%)
    pallas_call x1, Pallas kernels, per_device(): pl.pallas_call(functools.partial(mega, n_site), out_shape=(jax.ShapeDtype...  63.3 us
    pallas_call x1, Pallas kernels, per_device(): pl.pallas_call(store, out_shape=tuple((jax.ShapeDtypeStruct(r.shape, r.dt...  1.89 us

profile of v4, /device:TPU:1, one launch (start us, length us, event | category | flops | bytes accessed | tf_op | source)
XLA Modules:
  0.0 66.5 jit_solution(9478215041297279514)
XLA Ops:
  1.3 63.3 %column_move.1 = (bf16[1,6,128,128]{3,2,1,0:T(8,128)(2,1)}, bf16[2,1,6,128,128]{4,3,2,1,0:T(8,128)(2,1)}, f32[2,6,8,128]{3,2,1,0:T(8,128)}) custom-call(s32[1,96]{1,0:T(1,128)} %join_ref.1, f32[1]{0:T(128)S(6)} %copy.10.mom_ref, bf16[1,6,128,128]{3,2,1,0:T(8,128)(2,1)} %corner_ref.1, bf16[2,1,6,128,128]{4,3,2,1,0:T(8,128)(2,1)} %bcorner_ref.1, ...), custom_call_target="tpu_custom_call" | custom-call | tf_op jit(solution)/shard_map/column_move/pallas_call | solution.py:517
  64.6 1.9 %store.1 = (bf16[1,6,128,128]{3,2,1,0:T(8,128)(2,1)}, bf16[2,1,6,128,128]{4,3,2,1,0:T(8,128)(2,1)}, f32[2,6,8,128]{3,2,1,0:T(8,128)}) custom-call(bf16[1,6,128,128]{3,2,1,0:T(8,128)(2,1)} %get-tuple-element.6.refs_0_, bf16[2,1,6,128,128]{4,3,2,1,0:T(8,128)(2,1)} %get-tuple-element.7.refs_1_, f32[2,6,8,128]{3,2,1,0:T(8,128)} %get-tuple-element.8.refs_2_), custom_call_target="tpu_custom_call" | custom-call | tf_op jit(solution)/shard_map/store/pallas_call | solution.py:572

commit v5 on v4

--- a/solution.py
+++ b/solution.py
@@ -13,12 +13,12 @@
 NZ = 4
 HALVES = 2
 CHUNKS = (
+    (False, 0, (2,), 0),
     (True, 0, (1,), 0),
-    (False, 0, (2,), 0),
     (False, 1, (1,), 1),
     (True, 1, (2,), 1),
-    (True, 0, (0,), 1),
-    (False, 1, (0,), 2),
+    (False, 0, (0,), 2),
+    (True, 1, (0,), 2),
 )
 
 

time: 66.6 us -> 64.7 us (0.971)
  the two profiles are of different devices: /device:TPU:1 before, /device:TPU:24 now
where the time goes in v5:
time: 64.7 us; the launch traced here: 64.6 us
  Pallas kernels  63.3 us (98%)
  between operations  1.29 us (2%)
    pallas_call x1, Pallas kernels, per_device(): pl.pallas_call(functools.partial(mega, n_site), out_shape=(jax.ShapeDtype...  61.4 us
    pallas_call x1, Pallas kernels, per_device(): pl.pallas_call(store, out_shape=tuple((jax.ShapeDtypeStruct(r.shape, r.dt...  1.89 us

profile of v5, /device:TPU:24, one launch (start us, length us, event | category | flops | bytes accessed | tf_op | source)
XLA Modules:
  0.0 64.6 jit_solution(3303170518488854164)
XLA Ops:
  1.3 61.4 %column_move.1 = (bf16[1,6,128,128]{3,2,1,0:T(8,128)(2,1)}, bf16[2,1,6,128,128]{4,3,2,1,0:T(8,128)(2,1)}, f32[2,6,8,128]{3,2,1,0:T(8,128)}) custom-call(s32[1,96]{1,0:T(1,128)} %join_ref.1, f32[1]{0:T(128)S(6)} %copy.10.mom_ref, bf16[1,6,128,128]{3,2,1,0:T(8,128)(2,1)} %corner_ref.1, bf16[2,1,6,128,128]{4,3,2,1,0:T(8,128)(2,1)} %bcorner_ref.1, ...), custom_call_target="tpu_custom_call" | custom-call | tf_op jit(solution)/shard_map/column_move/pallas_call | solution.py:517
  62.7 1.9 %store.1 = (bf16[1,6,128,128]{3,2,1,0:T(8,128)(2,1)}, bf16[2,1,6,128,128]{4,3,2,1,0:T(8,128)(2,1)}, f32[2,6,8,128]{3,2,1,0:T(8,128)}) custom-call(bf16[1,6,128,128]{3,2,1,0:T(8,128)(2,1)} %get-tuple-element.6.refs_0_, bf16[2,1,6,128,128]{4,3,2,1,0:T(8,128)(2,1)} %get-tuple-element.7.refs_1_, f32[2,6,8,128]{3,2,1,0:T(8,128)} %get-tuple-element.8.refs_2_), custom_call_target="tpu_custom_call" | custom-call | tf_op jit(solution)/shard_map/store/pallas_call | solution.py:572

commit v6 on v5

--- a/solution.py
+++ b/solution.py
@@ -15,8 +15,8 @@
 CHUNKS = (
     (False, 0, (2,), 0),
     (True, 0, (1,), 0),
+    (True, 1, (2,), 1),
     (False, 1, (1,), 1),
-    (True, 1, (2,), 1),
     (False, 0, (0,), 2),
     (True, 1, (0,), 2),
 )

time: 64.7 us -> 64.5 us (level)
  no operation moved by 1% of the time
where the time goes in v6:
time: 64.5 us; the launch traced here: 64.4 us
  Pallas kernels  63.1 us (98%)
  between operations  1.29 us (2%)
    pallas_call x1, Pallas kernels, per_device(): pl.pallas_call(functools.partial(mega, n_site), out_shape=(jax.ShapeDtype...  61.2 us
    pallas_call x1, Pallas kernels, per_device(): pl.pallas_call(store, out_shape=tuple((jax.ShapeDtypeStruct(r.shape, r.dt...  1.89 us

profile of v6, /device:TPU:24, one launch (start us, length us, event | category | flops | bytes accessed | tf_op | source)
XLA Modules:
  0.0 64.4 jit_solution(3775320907241849640)
XLA Ops:
  1.3 61.2 %column_move.1 = (bf16[1,6,128,128]{3,2,1,0:T(8,128)(2,1)}, bf16[2,1,6,128,128]{4,3,2,1,0:T(8,128)(2,1)}, f32[2,6,8,128]{3,2,1,0:T(8,128)}) custom-call(s32[1,96]{1,0:T(1,128)} %join_ref.1, f32[1]{0:T(128)S(6)} %copy.10.mom_ref, bf16[1,6,128,128]{3,2,1,0:T(8,128)(2,1)} %corner_ref.1, bf16[2,1,6,128,128]{4,3,2,1,0:T(8,128)(2,1)} %bcorner_ref.1, ...), custom_call_target="tpu_custom_call" | custom-call | tf_op jit(solution)/shard_map/column_move/pallas_call | solution.py:517
  62.5 1.9 %store.1 = (bf16[1,6,128,128]{3,2,1,0:T(8,128)(2,1)}, bf16[2,1,6,128,128]{4,3,2,1,0:T(8,128)(2,1)}, f32[2,6,8,128]{3,2,1,0:T(8,128)}) custom-call(bf16[1,6,128,128]{3,2,1,0:T(8,128)(2,1)} %get-tuple-element.6.refs_0_, bf16[2,1,6,128,128]{4,3,2,1,0:T(8,128)(2,1)} %get-tuple-element.7.refs_1_, f32[2,6,8,128]{3,2,1,0:T(8,128)} %get-tuple-element.8.refs_2_), custom_call_target="tpu_custom_call" | custom-call | tf_op jit(solution)/shard_map/store/pallas_call | solution.py:572
